TPU v7x, 32 devices: a whole 2x2x4 slice. The times are simulated.
32 devices in a mesh: pb: 2 (over x), ka: 16 (over z, y, core).
Axes of the slice: x: 2, y: 2, z: 4, core: 2. Of those that a mesh axis runs over, the one named last changes fastest.
Arguments:
- coupling: bfloat16 [5120, 2, 2048], P('ka', 'pb'), may hold values from -0.009765625 to 0.009765625
- eigvec: float32 [16, 2048], P('ka'), may hold values from -0.75 to 0.75
- energies: float32 [16, 32], P('ka'), may hold values from -1 to 1
- k_coords: int32 [3, 16], replicated, may hold values from 0 to 63
- r_coords: int32 [3, 5120], P(None, 'ka'), may hold values from -12 to 12
- degeneracy: int32 [5120], P('ka'), may hold values from 1 to 8
- kq_index: int32 [16, 24], P('ka', 'pb'), may hold values from 0 to 15
- omega: float32 [24, 2], P('pb'), may hold values from 0.05 to 0.5
- phonon_modes: float32 [24, 2, 2], P('pb'), may hold values from -4 to 4
Outputs:
- sigma: float32 [16, 32], P('ka', 'pb')
All inputs are finite; a program needn't handle non-finite values.
Results may differ from a plain program's by a relative error of at most 0.0013.
Values may be sent and summed in bfloat16 or wider, within the bound.
No kernel may reach another device: no remote copies, remote signals or barrier semaphores. Data moves between devices by JAX's collectives and lax.ppermute only.
A program may use at most 64 MiB of HBM per device.

v0:
```python
import math

import jax
import jax.numpy as jnp
from jax import lax
from jax.sharding import PartitionSpec as P

KGRID = 64


THERMAL = 0.1
SMEARING = 0.05
HIGHEST = lax.Precision.HIGHEST


def phases(k_coords, r_coords, degeneracy):
    turns = (
        k_coords[0][:, None] * r_coords[0][None, :]
        + k_coords[1][:, None] * r_coords[1][None, :]
        + k_coords[2][:, None] * r_coords[2][None, :]
    ) % KGRID
    angle = turns.astype(jnp.float32) * (2.0 * math.pi / KGRID)
    inverse = 1.0 / degeneracy.astype(jnp.float32)
    cosine = (jnp.cos(angle) * inverse[None, :]).astype(jnp.bfloat16)
    sine = (jnp.sin(angle) * inverse[None, :]).astype(jnp.bfloat16)
    return (cosine, sine)


def combine_parts(cosine_sum, sine_sum, modes, square):
    cosine_rows = cosine_sum.reshape(cosine_sum.shape[0], modes, 2, square)
    sine_rows = sine_sum.reshape(sine_sum.shape[0], modes, 2, square)
    real_part = cosine_rows[:, :, 0] - sine_rows[:, :, 1]
    imag_part = cosine_rows[:, :, 1] + sine_rows[:, :, 0]
    return jnp.stack([real_part, imag_part], axis=2).reshape(
        cosine_sum.shape[0], modes * 2 * square
    )


def lorentz(spacing):
    return SMEARING / (math.pi * (spacing * spacing + SMEARING * SMEARING))


def self_energy(wannier, vector, energy, kq_vectors, kq_energies, omega, phonon):
    bands = energy.shape[0]
    modes = wannier.shape[0]
    matrix = wannier.astype(jnp.float32).reshape(modes, 2, bands, bands)
    rotate = vector.reshape(2, bands, bands)
    fold_real = jnp.einsum("vac,cn->van", matrix[:, 0], rotate[0], precision=HIGHEST) - jnp.einsum(
        "vac,cn->van", matrix[:, 1], rotate[1], precision=HIGHEST
    )
    fold_imag = jnp.einsum("vac,cn->van", matrix[:, 0], rotate[1], precision=HIGHEST) + jnp.einsum(
        "vac,cn->van", matrix[:, 1], rotate[0], precision=HIGHEST
    )
    mixed_real = jnp.einsum("qwv,wan->qvan", phonon, fold_real, precision=HIGHEST)
    mixed_imag = jnp.einsum("qwv,wan->qvan", phonon, fold_imag, precision=HIGHEST)
    target = kq_vectors.reshape(-1, 2, bands, bands)
    final_real = jnp.einsum(
        "qam,qvan->qmvn", target[:, 0], mixed_real, precision=HIGHEST
    ) + jnp.einsum("qam,qvan->qmvn", target[:, 1], mixed_imag, precision=HIGHEST)
    final_imag = jnp.einsum(
        "qam,qvan->qmvn", target[:, 0], mixed_imag, precision=HIGHEST
    ) - jnp.einsum("qam,qvan->qmvn", target[:, 1], mixed_real, precision=HIGHEST)
    strength = final_real * final_real + final_imag * final_imag
    fermi = 1.0 / (1.0 + jnp.exp(kq_energies / THERMAL))
    bose = 1.0 / jnp.expm1(omega / THERMAL)
    spacing = energy[None, None, None, :] - kq_energies[:, :, None, None]
    absorb = lorentz(spacing + omega[:, None, :, None])
    emit = lorentz(spacing - omega[:, None, :, None])
    bose_wide = bose[:, None, :, None]
    fermi_wide = fermi[:, :, None, None]
    occupy = (bose_wide + fermi_wide) * absorb + (bose_wide + 1.0 - fermi_wide) * emit
    return jnp.sum(strength * occupy, axis=(0, 1, 2))


def fourier_terms(k_coords, r_coords, degeneracy, slab, modes, square, count):
    cosine, sine = phases(k_coords, r_coords, degeneracy)
    stacked = jnp.dot(
        jnp.concatenate([cosine, sine], axis=0), slab, preferred_element_type=jnp.float32
    )
    return combine_parts(stacked[:count], stacked[count:], modes, square)


def shards(
    coupling, eigvec, energies, k_coords, r_coords, degeneracy, kq_index, omega, phonon_modes
):
    bands = energies.shape[1]
    points = eigvec.shape[0]
    local_modes = coupling.shape[1]
    slab = coupling.reshape(coupling.shape[0], -1)
    partial_value = lax.psum_scatter(
        fourier_terms(
            k_coords,
            r_coords,
            degeneracy,
            slab,
            local_modes,
            bands * bands,
            points * lax.axis_size("ka"),
        ),
        "ka",
        scatter_dimension=0,
        tiled=True,
    )
    own_wannier = partial_value.astype(jnp.bfloat16).reshape(points, local_modes, 2 * bands * bands)
    wannier = lax.all_gather(own_wannier, "pb", axis=1, tiled=True)
    pairs = kq_index.reshape(-1)
    pieces = (
        lax.all_gather(eigvec, "ka", axis=0, tiled=True),
        lax.all_gather(energies, "ka", axis=0, tiled=True),
    )
    labels = jnp.arange(pieces[0].shape[0], dtype=jnp.int32)
    hits = (pairs[:, None] == labels[None, :]).astype(jnp.float32)
    vectors_sum = jnp.dot(hits, pieces[0], precision=HIGHEST, preferred_element_type=jnp.float32)
    energy_sum = jnp.dot(hits, pieces[1], precision=HIGHEST, preferred_element_type=jnp.float32)
    kq_vectors = vectors_sum
    kq_energies = energy_sum
    queries = kq_index.shape[1]
    kq_vectors = kq_vectors.reshape(points, queries, eigvec.shape[1])
    kq_energies = kq_energies.reshape(points, queries, bands)

    def per_point(items):
        wannier_row, vector, energy, kq_rows, kq_levels = items
        return self_energy(wannier_row, vector, energy, kq_rows, kq_levels, omega, phonon_modes)

    sigma = lax.map(per_point, (wannier, eigvec, energies, kq_vectors, kq_energies))
    sigma = sigma / (queries * lax.axis_size("pb"))
    return lax.psum_scatter(sigma, "pb", scatter_dimension=1, tiled=True)


def solution(mesh):
    in_specs = (
        P("ka", "pb", None),
        P("ka", None),
        P("ka", None),
        P(),
        P(None, "ka"),
        P("ka"),
        P("ka", "pb"),
        P("pb", None),
        P("pb", None, None),
    )
    out_specs = P("ka", "pb")
    return jax.shard_map(shards, mesh=mesh, in_specs=in_specs, out_specs=out_specs, check_vma=False)
```

profile of v0, /device:TPU:0, one launch (start us, length us, event | category | flops | bytes accessed | tf_op | source)
XLA Modules:
  0.0 140.0 jit_solution(4159584743243929971)
XLA Ops:
  6.5 0.8 broadcast_add_fusion.1
  7.3 0.8 copy.45
  8.1 0.8 slice_reduce_fusion.4
  8.9 0.8 slice_bitcast_fusion.14
  9.7 0.7 convert_divide_fusion
  10.4 0.2 multiply_convert_fusion.1
  10.6 0.3 fusion
  11.2 0.1 slice_subtract_fusion
  11.4 0.1 pad_maximum_fusion
  11.6 63.8 %all-reduce.2 = bf16[16,2048]{1,0:T(8,128)(2,1)S(1)} all-reduce(f32[16,2048]{1,0:T(8,128)S(1)} %bitcast.78), channel_id=3, replica_groups=mesh['pb'=2,'ka'=16] {'ka'}, use_global_device_ids=true, to_apply=%region_0.1.clone | all-reduce | flops 32768 | bytes 196608
  75.4 0.6 dynamic-slice.2
  76.0 0.7 fusion.28
  76.6 4.4 %all-gather.2 = bf16[2,1,2048]{2,1,0:T(2,128)(2,1)S(1)} all-gather(bf16[1,1,2048]{2,1,0:T(2,128)(2,1)S(1)} %fusion.28), channel_id=2, replica_groups=mesh['pb'=2,'ka'=16] {'pb'}, dimensions={0}, use_global_device_ids=true | all-gather | bytes 12288 | tf_op jit(solution)/shard_map/all_gather | solution.py:105
  81.3 0.1 fusion.27
  81.5 0.1 fusion.26
  81.6 0.1 fusion.8
  81.8 17.5 %all-gather.1 = f32[16,1,2048]{2,1,0:T(1,128)S(1)} all-gather(f32[1,1,2048]{2,1,0:T(1,128)S(1)} %bitcast.80), channel_id=1, replica_groups=mesh['pb'=2,'ka'=16] {'ka'}, dimensions={0}, use_global_device_ids=true | all-gather | bytes 139264 | tf_op jit(solution)/shard_map/all_gather | solution.py:108
  99.3 0.3 fusion.15
  99.5 0.1 reshape.87
  99.7 0.1 fusion.7
  99.8 0.6 convolution_bitcast_fusion.1
  100.4 0.6 convolution_bitcast_fusion
  101.1 0.7 fusion.13
  101.8 0.7 fusion.9
  102.5 0.7 fusion.2
  103.2 19.1 %all-gather.3 = f32[16,1,32]{2,1,0:T(1,128)S(1)} all-gather(f32[1,1,32]{2,1,0:T(1,128)S(1)} %bitcast.83), channel_id=1, replica_groups=mesh['pb'=2,'ka'=16] {'ka'}, dimensions={0}, use_global_device_ids=true | all-gather | bytes 2176 | tf_op jit(solution)/shard_map/all_gather | solution.py:109
  122.2 0.2 add_divide_fusion
  122.6 0.1 broadcast_subtract_fusion
  122.9 1.0 fusion.6
  123.8 0.7 copy.55
  124.5 7.3 %reduce-scatter.4.cloned.1.call-done = f32[16,1]{1,0:T(8,128)} async-done(((f32[32,1]{1,0:T(8,128)}), f32[16,1]{1,0:T(8,128)}) %reduce-scatter.4.cloned.1.call-update) | async-done | bytes 80
  131.9 1.3 copy.56
  (27 shorter events, 0.9 us)
Async XLA Ops:
  6.5 4.1 %copy-start = (bf16[320,1,2048]{2,0,1:T(8,128)(2,1)S(1)}, bf16[320,1,2048]{2,0,1:T(8,128)(2,1)}, u32[]{:S(2)}) copy-start(bf16[320,1,2048]{2,0,1:T(8,128)(2,1)} %param.9) | copy-start | bytes 3932164
  6.5 125.3 %reduce-scatter.4.cloned.1.call-start = ((), (), s32[]{:S(2)}) async-start(), calls=%async_computation.1 | async-start | bytes 24576
  10.9 64.4 %copy-start.5 = (u32[32]{0:T(128)S(1)}, u32[32]{0:T(128)}, u32[]{:S(2)}) copy-start(u32[32]{0:T(128)} %constant.68) | copy-start | bytes 388
  10.9 70.2 %copy-start.1 = (f32[1,2048]{1,0:T(1,128)S(1)}, f32[1,2048]{1,0:T(1,128)}, u32[]{:S(2)}) copy-start(f32[1,2048]{1,0:T(1,128)} %param.10) | copy-start | bytes 24580
  11.0 88.3 %copy-start.4 = (s32[1,12]{1,0:T(1,128)S(1)}, s32[1,12]{1,0:T(1,128)}, u32[]{:S(2)}) copy-start(s32[1,12]{1,0:T(1,128)} %param.15) | copy-start | bytes 148
  11.2 88.6 %copy-start.2 = (f32[12,2,2]{0,2,1:T(2,128)S(1)}, f32[12,2,2]{0,2,1:T(2,128)}, u32[]{:S(2)}) copy-start(f32[12,2,2]{0,2,1:T(2,128)} %param.17) | copy-start | bytes 580
  101.8 1.4 copy-start.3
Sparse Core Ops, SparseCore 0:
  124.7 7.1 reduce-scatter.3
where the time goes:
time: 140 us
  blocking collectives  105 us (75%)
  between operations  13.6 us (10%)
  waiting for transfers between devices  7.35 us (5%)
  local copies, waits for them, and re-layouts  6.51 us (5%)
  matrix products  5.57 us (4%)
  other arithmetic  2.19 us (2%)
    unnamed x1, blocking collectives  63.8 us
    all_gather x1, blocking collectives, shards(): lax.all_gather(energies, 'ka', axis=0, tiled=True)  19.1 us
    all_gather x1, blocking collectives, shards(): lax.all_gather(eigvec, 'ka', axis=0, tiled=True)  17.5 us
    unnamed x2, waiting for transfers between devices  7.35 us
    all_gather x1, blocking collectives, shards(): wannier = lax.all_gather(own_wannier, 'pb', axis=1, tiled=True)  4.36 us
    unnamed x18, local copies, waits for them, and re-layouts  4.06 us
  transfers between devices with their start and end apart: 1, of which 1 were waited for; matrix products, arithmetic and copies ran while one was open for 0% of the time, Pallas kernels for 0%

commit v1 on v0

v1 whole, which is shorter than its diff:
```python
import math

import jax
import jax.numpy as jnp
from jax import lax
from jax.sharding import PartitionSpec as P

KGRID = 64


THERMAL = 0.1
SMEARING = 0.05
HIGHEST = lax.Precision.HIGHEST


def phases(k_coords, r_coords, degeneracy):
    turns = (
        k_coords[0][:, None] * r_coords[0][None, :]
        + k_coords[1][:, None] * r_coords[1][None, :]
        + k_coords[2][:, None] * r_coords[2][None, :]
    ) % KGRID
    angle = turns.astype(jnp.float32) * (2.0 * math.pi / KGRID)
    inverse = 1.0 / degeneracy.astype(jnp.float32)
    cosine = (jnp.cos(angle) * inverse[None, :]).astype(jnp.bfloat16)
    sine = (jnp.sin(angle) * inverse[None, :]).astype(jnp.bfloat16)
    return (cosine, sine)


def lorentz(spacing):
    return SMEARING / (math.pi * (spacing * spacing + SMEARING * SMEARING))


def fourier_terms(k_coords, r_coords, degeneracy, slab, modes, square):
    cosine, sine = phases(k_coords, r_coords, degeneracy)
    count = cosine.shape[0]
    stacked = jnp.dot(
        jnp.concatenate([cosine, sine], axis=0), slab, preferred_element_type=jnp.float32
    ).reshape(2, count, modes, 2, square)
    real_part = stacked[0, :, :, 0] - stacked[1, :, :, 1]
    imag_part = stacked[0, :, :, 1] + stacked[1, :, :, 0]
    return jnp.stack([real_part, imag_part], axis=2).reshape(count, modes * 2 * square)


def self_energy(wannier, vector, energy, vectors, levels, kq_index, omega, phonon):
    matrix = wannier.astype(jnp.float32)

    def fold(x, y):
        return jnp.einsum("wac,cn->wan", x, y, precision=HIGHEST)

    fold_real = fold(matrix[:, 0], vector[0]) - fold(matrix[:, 1], vector[1])
    fold_imag = fold(matrix[:, 0], vector[1]) + fold(matrix[:, 1], vector[0])
    right = jnp.stack(
        [jnp.stack([fold_real, fold_imag]), jnp.stack([fold_imag, -fold_real])], axis=0
    )
    whole = jnp.einsum("kram,rswan->kmswn", vectors, right, precision=HIGHEST)
    points, bands = levels.shape
    table = jnp.concatenate([whole.reshape(points, -1), levels], axis=1)
    hits = (kq_index[:, None] == jnp.arange(points)[None, :]).astype(jnp.float32)
    rows = jnp.dot(hits, table, precision=HIGHEST, preferred_element_type=jnp.float32)
    kq_levels = rows[:, -bands:]
    picked = rows[:, :-bands].reshape((rows.shape[0],) + whole.shape[1:])
    final = jnp.einsum("qmswn,qwv->qsvmn", picked, phonon, precision=HIGHEST)
    strength = final[:, 0] * final[:, 0] + final[:, 1] * final[:, 1]
    fermi = 1.0 / (1.0 + jnp.exp(kq_levels / THERMAL))
    bose = 1.0 / jnp.expm1(omega / THERMAL)
    spacing = energy[None, None, None, :] - kq_levels[:, None, :, None]
    shift = omega[:, :, None, None]
    bose_wide = bose[:, :, None, None]
    fermi_wide = fermi[:, None, :, None]
    occupy = (bose_wide + fermi_wide) * lorentz(spacing + shift) + (
        bose_wide + 1.0 - fermi_wide
    ) * lorentz(spacing - shift)
    return jnp.sum(strength * occupy, axis=(0, 1, 2)) / kq_index.shape[0]


def shards(
    coupling, eigvec, energies, k_coords, r_coords, degeneracy, kq_index, omega, phonon_modes
):
    points, bands = energies.shape
    local_modes = coupling.shape[1]
    square = bands * bands
    groups = lax.axis_size("pb")
    holders = lax.axis_size("ka")
    group = lax.axis_index("pb")
    slab = coupling.reshape(coupling.shape[0], -1)
    partial_value = fourier_terms(k_coords, r_coords, degeneracy, slab, local_modes, square)
    partial_value = partial_value.reshape(holders, -1)
    share = eigvec.reshape(groups, -1)
    share = lax.dynamic_index_in_dim(share, group, 0, keepdims=False)
    extras = [share, energies.reshape(-1), kq_index.astype(jnp.float32).reshape(-1)]
    extras += [omega.reshape(-1), phonon_modes.reshape(-1)]
    sizes = [x.shape[0] for x in extras]
    tail = jnp.concatenate(extras)
    sums = partial_value.shape[1]
    length = -(-(sums + tail.shape[0]) // 128) * 128
    tail = jnp.pad(tail, (0, length - sums - tail.shape[0]))
    parcel = jnp.concatenate(
        [partial_value, jnp.broadcast_to(tail[None], (holders, tail.shape[0]))], axis=1
    )
    parcel = jnp.broadcast_to(parcel[None], (groups, holders, length))
    got = lax.all_to_all(
        parcel.reshape(groups * holders, length // 128, 128), ("pb", "ka"), 0, 0, tiled=True
    ).reshape(groups, holders, length)
    own = lax.axis_index("ka")
    wannier = jnp.sum(got[:, :, :sums], axis=1).astype(jnp.bfloat16)
    wannier = wannier.reshape(groups, points, local_modes, 2, bands, bands)
    fields = []
    start = sums
    for size in sizes:
        fields.append(got[:, :, start : start + size])
        start += size
    all_vectors = jnp.swapaxes(fields[0], 0, 1).reshape(holders * points, 2, bands, bands)
    all_levels = fields[1][0].reshape(holders * points, bands)
    targets = lax.dynamic_index_in_dim(fields[2], own, 1, keepdims=False)
    targets = targets.reshape(groups, points, -1).astype(jnp.int32)
    all_omega = fields[3][:, 0].reshape((-1,) + omega.shape[1:])
    all_phonon = fields[4][:, 0].reshape((-1,) + phonon_modes.shape[1:])
    width = bands // groups
    results = []
    for point in range(points):
        vector = eigvec[point].reshape(2, bands, bands)
        results.append(
            self_energy(
                wannier[:, point].reshape(groups * local_modes, 2, bands, bands),
                lax.dynamic_slice_in_dim(vector, group * width, width, 2),
                lax.dynamic_slice_in_dim(energies[point], group * width, width, 0),
                all_vectors.reshape(-1, 2, bands, bands),
                all_levels,
                targets[:, point].reshape(-1),
                all_omega,
                all_phonon,
            )
        )
    return jnp.stack(results)


def solution(mesh):
    in_specs = (
        P("ka", "pb", None),
        P("ka", None),
        P("ka", None),
        P(),
        P(None, "ka"),
        P("ka"),
        P("ka", "pb"),
        P("pb", None),
        P("pb", None, None),
    )
    out_specs = P("ka", "pb")
    return jax.shard_map(shards, mesh=mesh, in_specs=in_specs, out_specs=out_specs, check_vma=False)
```

time: 140 us -> 47.2 us (0.34)
  blocking collectives: 105 us -> 0 us
  between operations: 13.6 us -> 0.26 us
  waiting for transfers between devices: 7.35 us -> 15.7 us
  starting transfers between devices: 0.01 us -> 7.33 us
  local copies, waits for them, and re-layouts: 6.51 us -> 12.1 us
  other arithmetic: 2.19 us -> 4.32 us
  matrix products: 5.57 us -> 7.04 us
    unnamed x1 -> x0, blocking collectives: 63.8 us -> none
    all_gather x3 -> x0, blocking collectives: 40.9 us -> none  [the longest x1 19.1 us: shards(): lax.all_gather(energies, 'ka', axis=0, tiled=True)]
    all_to_all x0 -> x1, waiting for transfers between devices: none -> 15.7 us  [shards(): lax.all_to_all(parcel.reshape(groups * holders, length // 128, 128), ('pb...]
    unnamed x2 -> x0, waiting for transfers between devices: 7.35 us -> none
    all_to_all x0 -> x1, starting transfers between devices: none -> 7.33 us  [shards(): lax.all_to_all(parcel.reshape(groups * holders, length // 128, 128), ('pb...]
    reshape x4 -> x9, local copies, waits for them, and re-layouts: 0.45 us -> 5.8 us  [the longest x2 2.89 us: self_energy(): picked = rows[:, :-bands].reshape((rows.shape[0],) + whole.shape[1:])]
    unnamed x18 -> x8, local copies, waits for them, and re-layouts: 4.06 us -> 2.12 us
    dot_general x12 -> x7, matrix products: 5.24 us -> 5.4 us  [the longest x1 3.34 us: self_energy(): final = jnp.einsum('qmswn,qwv->qsvmn', picked, phonon, precision=HIGHEST)]
where the time goes in v1:
time: 47.2 us; the launch traced here: 46.8 us
  waiting for transfers between devices  15.7 us (33%)
  local copies, waits for them, and re-layouts  12.1 us (26%)
  starting transfers between devices  7.33 us (16%)
  matrix products  7.04 us (15%)
  other arithmetic  4.32 us (9%)
    all_to_all x1, waiting for transfers between devices, shards(): lax.all_to_all(parcel.reshape(groups * holders, length // 128, 128), ('pb...  15.7 us
    all_to_all x1, starting transfers between devices, shards(): lax.all_to_all(parcel.reshape(groups * holders, length // 128, 128), ('pb...  7.33 us
    dot_general x1, matrix products, self_energy(): final = jnp.einsum('qmswn,qwv->qsvmn', picked, phonon, precision=HIGHEST)  3.34 us
    reshape x2, local copies, waits for them, and re-layouts, self_energy(): picked = rows[:, :-bands].reshape((rows.shape[0],) + whole.shape[1:])  2.89 us
    unnamed x8, local copies, waits for them, and re-layouts  2.12 us
    dot_general x1, matrix products, fourier_terms(): jnp.dot(jnp.concatenate([cosine, sine], axis=0), slab, preferred_element_...  1.64 us
    reshape x1, local copies, waits for them, and re-layouts, self_energy(): table = jnp.concatenate([whole.reshape(points, -1), levels], axis=1)  1.54 us
    unnamed x1, other arithmetic  1.36 us
  transfers between devices with their start and end apart: 1, of which 1 were waited for; matrix products, arithmetic and copies ran while one was open for 0% of the time, Pallas kernels for 0%

profile of v1, /device:TPU:0, one launch (start us, length us, event | category | flops | bytes accessed | tf_op | source)
XLA Modules:
  0.0 46.8 jit_solution(15864475407212788428)
XLA Ops:
  0.0 0.7 %convert_bitcast_fusion = f32[12]{0:T(128)S(1)} fusion(s32[1,12]{1,0:T(1,128)} %param.15), kind=kLoop, calls=%fused_computation.78 | loop fusion | flops 12 | bytes 96 | tf_op jit(solution)/shard_map/reshape | solution.py:90
  0.7 0.8 %slice_bitcast_fusion.10 = (s32[16]{0:T(128)S(1)}, s32[16]{0:T(128)S(1)}, s32[16]{0:T(128)S(1)}) fusion(s32[3,16]{1,0:T(4,128)} %param.12), kind=kLoop, calls=%fused_computation.81 | loop fusion | bytes 384 | tf_op jit(solution)/shard_map/mul | solution.py:18
  1.5 0.7 %convert_divide_fusion = f32[320]{0:T(512)S(1)} fusion(s32[320]{0:T(512)} %param.14), kind=kLoop, calls=%fused_computation.61 | loop fusion | flops 640 | bytes 2560 | tf_op jit(solution)/shard_map/div | solution.py:23
  2.1 0.8 %slice_reduce_fusion.3 = (s32[320]{0:T(512)S(1)}, s32[320]{0:T(512)S(1)}, s32[320]{0:T(512)S(1)}) fusion(s32[3,320]{1,0:T(4,128)} %param.13), kind=kLoop, calls=%fused_computation.64 | loop fusion | bytes 7680 | tf_op jit(solution)/shard_map/slice | solution.py:18
  3.0 0.5 %broadcast.133 = f32[]{:T(128)} broadcast(f32[]{:T(128)} %constant.91), dimensions={} | broadcast | bytes 8 | tf_op args[1]
  3.5 1.4 %reduce.23 = f32[2048]{0:T(1024)S(1)} reduce(f32[1,2048]{1,0:T(1,128)} %param.10, f32[]{:T(128)} %broadcast.133), dimensions={0}, to_apply=%param.10.reduce_sub_computation.5 | reduce | bytes 16388 | tf_op args[1]
  4.9 0.8 %copy.36 = f32[12,2]{1,0:T(8,128)S(1)} copy(f32[12,2]{0,1:T(2,128)} %param.16) | data formatting | bytes 192 | tf_op args[7]
  5.7 0.8 %copy.37 = f32[12,2,2]{2,1,0:T(2,128)S(1)} copy(f32[12,2,2]{0,2,1:T(2,128)} %param.17) | data formatting | bytes 384 | tf_op args[8]
  6.6 0.7 %concatenate.13 = f32[1140]{0:T(1024)S(1)} concatenate(f32[1024]{0:T(1024)S(1)} %bitcast.115, f32[32]{0:T(128)} %bitcast.116, f32[12]{0:T(128)S(1)} %convert_bitcast_fusion, f32[24]{0:T(128)S(1)} %reshape.152, f32[48]{0:T(128)S(1)} %reshape.153), dimensions={0} | concatenate | bytes 9120 | tf_op jit(solution)/shard_map/concatenate | solution.py:93
  7.4 0.2 multiply_convert_fusion.1
  7.6 1.6 %fusion = f32[2,16,2,1024]{3,1,2,0:T(8,128)S(1)} fusion(bf16[2,16,320,1]{2,1,3,0:T(8,128)(2,1)S(1)} %bitcast.113, bf16[40,2,8,1024]{3,2,1,0:T(8,128)(2,1)} %bitcast.107), kind=kOutput, calls=%fused_computation.1 | convolution fusion | flops 41943040 | bytes 1593344 | tf_op jit(solution)/shard_map/dot_general | solution.py:36
  9.3 0.1 copy.35
  9.5 0.9 %reshape.154 = f32[32,25,128]{2,1,0:T(8,128)} reshape(f32[2,16,3200]{2,1,0:T(8,128)S(1)} %broadcast_in_dim.5) | data formatting | bytes 819200 | tf_op jit(solution)/shard_map/reshape | solution.py:102
  10.4 7.3 %all-to-all-start = ((f32[32,25,128]{2,1,0:T(8,128)}), f32[32,25,128]{2,1,0:T(8,128)S(1)}, u32[]{:S(2)}, u32[]{:S(2)}) async-start(f32[32,25,128]{2,1,0:T(8,128)} %reshape.154), calls=%async_computation | async-start | bytes 1048576 | tf_op jit(solution)/shard_map/all_to_all | solution.py:101
  17.9 15.7 %all-to-all-done = f32[32,25,128]{2,1,0:T(8,128)S(1)} async-done(((f32[32,25,128]{2,1,0:T(8,128)}), f32[32,25,128]{2,1,0:T(8,128)S(1)}, u32[]{:S(2)}, u32[]{:S(2)}) %all-to-all-start) | async-done | bytes 409632 | tf_op jit(solution)/shard_map/all_to_all | solution.py:101
  34.1 0.1 copy.38
  34.3 0.2 fusion.21
  34.6 0.3 fusion.22
  34.9 0.3 fusion.2
  35.2 0.3 convolution_subtract_fusion
  35.6 0.2 reshape.163
  35.8 0.6 %convolution_bitcast_fusion = f32[16,32,2,2,16]{1,4,3,2,0:T(8,128)S(1)} fusion(f32[16,2,32,32,1,1]{3,2,1,0,4,5:T(8,128)S(1)} %reshape.163, f32[1,2,2,32,16]{3,4,2,1,0:T(8,128)S(1)} %get-tuple-element.11, f32[1,2,2,32,16]{3,4,2,1,0:T(8,128)S(1)} %get-tuple-element.10), kind=kOutput, calls=%fused_computation.3 | convolution fusion | flops 25169920 | bytes 278528 | tf_op jit(solution)/shard_map/kram,rswan->kmswn/dot_general | solution.py:55
  36.4 0.7 %copy.43 = f32[16,32,2,2,16]{4,3,2,1,0:T(2,128)S(1)} copy(f32[16,32,2,2,16]{1,4,3,2,0:T(8,128)S(1)} %convolution_bitcast_fusion) | data formatting | bytes 262144 | tf_op jit(solution)/shard_map/kram,rswan->kmswn/dot_general | solution.py:55
  37.2 1.5 %reshape.157 = f32[16,2048]{1,0:T(8,128)S(1)} reshape(f32[16,32,2,2,16]{4,3,2,1,0:T(2,128)S(1)} %copy.43) | data formatting | bytes 262144 | tf_op jit(solution)/shard_map/reshape | solution.py:57
  38.7 0.3 fusion.8
  39.1 0.1 reshape_squeeze.9
  39.3 2.1 %reshape.158 = f32[24,32,2,2,16]{4,3,2,1,0:T(2,128)S(1)} reshape(f32[24,2048]{1,0:T(8,128)S(1)} %slice.119) | data formatting | bytes 393216 | tf_op jit(solution)/shard_map/reshape | solution.py:61
  41.4 0.8 %copy.45 = f32[24,32,2,2,16]{1,3,4,2,0:T(2,128)S(1)} copy(f32[24,32,2,2,16]{4,3,2,1,0:T(2,128)S(1)} %reshape.158) | data formatting | bytes 393216 | tf_op jit(solution)/shard_map/reshape | solution.py:61
  42.2 3.3 %fusion.19 = f32[24,2,32,2,16]{2,1,4,3,0:T(2,128)S(1)} fusion(f32[24,32,2,2,16]{1,3,4,2,0:T(2,128)S(1)} %copy.45, f32[24,2,2]{2,1,0:T(2,128)S(1)} %reshape_squeeze.9), kind=kOutput, calls=%fused_computation.40 | convolution fusion | flops 1179648 | bytes 393600 | tf_op jit(solution)/shard_map/qmswn,qwv->qsvmn/dot_general | solution.py:62
  45.7 0.1 broadcast_add_fusion
  45.8 0.4 fusion.7
  46.2 0.5 %multiply_bitcast_fusion = f32[1,16]{1,0:T(1,128)} fusion(f32[16]{0:T(128)S(1)} %fusion.7), kind=kLoop, calls=%fused_computation.77 | loop fusion | flops 16 | bytes 128 | tf_op jit(solution)/shard_map/div | solution.py:73
  (36 shorter events, 1.5 us)
Async XLA Ops:
  9.5 8.3 %copy-start = (f32[1,2048]{1,0:T(1,128)S(1)}, f32[1,2048]{1,0:T(1,128)}, u32[]{:S(2)}) copy-start(f32[1,2048]{1,0:T(1,128)} %param.10) | copy-start | bytes 24580
  9.5 8.3 %copy-start.1 = (f32[1,32]{1,0:T(1,128)S(1)}, f32[1,32]{1,0:T(1,128)}, u32[]{:S(2)}) copy-start(f32[1,32]{1,0:T(1,128)} %param.11) | copy-start | bytes 388
  10.4 23.2 %all-to-all-start = ((f32[32,25,128]{2,1,0:T(8,128)}), f32[32,25,128]{2,1,0:T(8,128)S(1)}, u32[]{:S(2)}, u32[]{:S(2)}) async-start(f32[32,25,128]{2,1,0:T(8,128)} %reshape.154), calls=%async_computation | async-start | bytes 1048576 | tf_op jit(solution)/shard_map/all_to_all | solution.py:101

commit v2 on v0

v2 whole, which is shorter than its diff:
```python
import functools
import math

import jax
import jax.numpy as jnp
from jax import lax
from jax.experimental import pallas as pl
from jax.experimental.pallas import tpu as pltpu
from jax.sharding import PartitionSpec as P

KGRID = 64
LANES = 128
HALF = LANES // 2

THERMAL = 0.1
SMEARING = 0.05
HIGHEST = lax.Precision.HIGHEST
F32 = jnp.float32
BF16 = jnp.bfloat16
VMEM = pl.BlockSpec(memory_space=pltpu.VMEM)
SMEM = pl.BlockSpec(memory_space=pltpu.SMEM)


def wave(turns):
    quarter = KGRID // 4
    turn = turns & (KGRID - 1)
    quadrant = (turn + quarter // 2) // quarter
    angle = (turn - quadrant * quarter).astype(F32) * (2.0 * math.pi / KGRID)
    square = angle * angle
    near = 1.0 + square * (
        -1 / 2 + square * (1 / 24 + square * (-1 / 720 + square * (1 / 40320)))
    )
    far = angle * (
        1.0 + square * (-1 / 6 + square * (1 / 120 + square * (-1 / 5040 + square * (1 / 362880))))
    )
    odd = (quadrant & 1) == 1
    cosine = jnp.where(odd, far, near)
    sine = jnp.where(odd, near, far)
    cosine = jnp.where(((quadrant + 1) & 2) == 2, -cosine, cosine)
    sine = jnp.where((quadrant & 2) == 2, -sine, sine)
    return cosine, sine


def pack_kernel(
    groups, place, k_ref, r_ref, degeneracy_ref, coupling_ref, vector_ref, energy_ref,
    index_ref, omega_ref, phonon_ref, out_ref, rows_ref, extra_ref,
):
    count = k_ref.shape[1]
    width = coupling_ref.shape[1]
    tiles = width // LANES
    share = tiles // groups
    turns = lax.dot_general(
        k_ref[...].astype(F32), r_ref[...].astype(F32), (((0,), (0,)), ((), ())),
        preferred_element_type=F32, precision=HIGHEST,
    ).astype(jnp.int32)
    cosine, sine = wave(turns)
    inverse = 1.0 / degeneracy_ref[...].astype(F32)
    both = jnp.concatenate([cosine * inverse, sine * inverse], axis=0).astype(BF16)
    step = 2 * LANES
    for start in range(0, width // 2, step):
        left = jnp.dot(both, coupling_ref[:, start : start + step], preferred_element_type=F32)
        other = start + width // 2
        right = jnp.dot(both, coupling_ref[:, other : other + step], preferred_element_type=F32)
        real = left[:count] - right[count:]
        imag = right[:count] + left[count:]
        for piece in range(step // LANES):
            tile = start // LANES + piece
            lanes = slice(piece * LANES, (piece + 1) * LANES)
            rows_ref[pl.ds(tile, count, tiles), :] = real[:, lanes]
            rows_ref[pl.ds(tile + tiles // 2, count, tiles), :] = imag[:, lanes]
    extra_ref[...] = jnp.zeros_like(extra_ref)
    bands, queries, modes = energy_ref.shape[1], index_ref.shape[1], omega_ref.shape[0]
    extra_ref[0:1, :bands] = energy_ref[...]
    extra_ref[1:2, :queries] = index_ref[...].astype(F32)
    extra_ref[2 : 2 + modes, :queries] = omega_ref[...]
    for mode in range(phonon_ref.shape[0]):
        first = 2 + modes * (1 + mode)
        extra_ref[first : first + modes, :queries] = phonon_ref[mode]
    extra = extra_ref[...]
    high = extra.astype(BF16).astype(F32)
    low = pltpu.roll(extra - high, HALF, 1)
    lane = lax.broadcasted_iota(jnp.int32, extra.shape, 1)
    extra = jnp.where(lane < HALF, high, low)
    mine = vector_ref[0:share, :]
    for group in range(1, groups):
        mine = jnp.where(place[0] == group, vector_ref[group * share : (group + 1) * share, :], mine)
    tail = jnp.concatenate([mine, extra], axis=0).astype(BF16)
    for row in range(count):
        block = rows_ref[row * tiles : (row + 1) * tiles, :].astype(BF16)
        for group in range(groups):
            out_ref[group * count + row, :tiles, :] = block
            out_ref[group * count + row, tiles:, :] = tail


def split(value):
    high = value.astype(BF16)
    return high, (value - high.astype(F32)).astype(BF16)


def energy_kernel(
    groups, bands, queries, place, got_ref, vector_ref, energy_ref, out_ref,
    turned_ref, level_ref, index_ref, scalar_ref, semaphore,
):
    own_group, own_holder = place[0], place[1]
    holders = got_ref.shape[0] // groups
    tiles = 2 * bands * bands // LANES
    share = tiles // groups
    fold = LANES // bands
    half = tiles // 2
    modes = groups
    width = bands // groups
    begin = tiles + share
    for group in range(groups):
        row = got_ref[group * holders + own_holder, begin : begin + 8, :].astype(F32)
        index_ref[group] = row.astype(jnp.int32)
    copy = pltpu.make_async_copy(index_ref, scalar_ref, semaphore)
    copy.start()
    lane = lax.broadcasted_iota(jnp.int32, (8, LANES), 1)
    slot = lane // bands
    stack = []
    for mode in range(modes):
        total = got_ref[mode * holders, :tiles, :].astype(F32)
        for holder in range(1, holders):
            total = total + got_ref[mode * holders + holder, :tiles, :].astype(F32)
        for part in range(2):
            block = total[part * half : (part + 1) * half]
            for piece in range(fold):
                stack.append(block[:, piece * bands : (piece + 1) * bands])
    matrix = jnp.concatenate(stack, axis=0)
    vector = vector_ref[:, :, :width]
    for group in range(1, groups):
        other = vector_ref[:, :, group * width : (group + 1) * width]
        vector = jnp.where(own_group == group, other, vector)
    with_real = jnp.dot(matrix, vector[0], precision=HIGHEST, preferred_element_type=F32)
    with_imag = jnp.dot(matrix, vector[1], precision=HIGHEST, preferred_element_type=F32)
    reals, imags = [], []
    for mode in range(modes):
        top = slice(2 * mode * bands, (2 * mode + 1) * bands)
        low = slice((2 * mode + 1) * bands, (2 * mode + 2) * bands)
        reals.append(with_real[top] - with_imag[low])
        imags.append(with_imag[top] + with_real[low])
    folded = jnp.concatenate(
        [
            jnp.concatenate(reals + imags, axis=1),
            jnp.concatenate(imags + [-x for x in reals], axis=1),
        ],
        axis=0,
    )
    left = folded.T
    left_high, left_low = split(left)
    for holder in range(holders):
        tile = [
            got_ref[group * holders + holder, tiles : tiles + share, :].astype(F32)
            for group in range(groups)
        ]
        tile = jnp.concatenate(tile, axis=0) if groups > 1 else tile[0]
        turned_ref[0, holder] = tile
        for turn in range(1, fold):
            turned_ref[turn, holder] = pltpu.roll(tile, turn * bands, 1)
        row = got_ref[holder, begin : begin + 8, :].astype(F32)
        row = jnp.where(lane < HALF, row + pltpu.roll(row, HALF, 1), 0.0)
        row = jnp.where(slot < 1, row, 0.0)
        full = row
        for turn in range(1, fold):
            full = full + pltpu.roll(row, turn * bands, 1)
        level_ref[holder] = full
    span = queries * bands
    source = lax.broadcasted_iota(jnp.int32, (LANES, span), 0) % HALF
    target = lax.broadcasted_iota(jnp.int32, (LANES, span), 1) // bands
    spread = jnp.where(source == target, 1.0, 0.0).astype(BF16)
    down = lax.broadcasted_iota(jnp.int32, (width, bands), 0) + own_group * width
    across = lax.broadcasted_iota(jnp.int32, (width, bands), 1)
    energy = jnp.sum(jnp.where(down == across, energy_ref[...], 0.0), axis=1, keepdims=True)
    copy.wait()
    total = jnp.zeros((width, LANES), F32)
    for group in range(groups):
        table = jnp.dot(
            got_ref[group * holders, begin:, :], spread, preferred_element_type=F32
        )
        for start in range(0, queries, fold):
            points = [scalar_ref[group, 1, start + item] for item in range(fold)]
            level = level_ref[points[0]]
            for item in range(1, fold):
                level = jnp.where(slot == item, level_ref[points[item]], level)
            level = level[0:1]
            blocks = []
            for part in range(2):
                for piece in range(fold):
                    rows = slice(part * half, (part + 1) * half)
                    block = turned_ref[(-piece) % fold, points[0], rows, :]
                    for item in range(1, fold):
                        block = jnp.where(
                            slot[:half] == item,
                            turned_ref[(item - piece) % fold, points[item], rows, :],
                            block,
                        )
                    blocks.append(block)
            chosen = jnp.concatenate(blocks, axis=0).astype(BF16)
            whole = jnp.dot(left_high, chosen, preferred_element_type=F32) + jnp.dot(
                left_low, chosen, preferred_element_type=F32
            )
            values = table[:, start * bands : (start + fold) * bands]
            fermi = 1.0 / (1.0 + jnp.exp(level / THERMAL))
            spacing = energy - level
            for out_mode in range(modes):
                real = imag = None
                for mode in range(modes):
                    row = 2 + modes * (1 + mode) + out_mode
                    weight = values[row : row + 1]
                    one = whole[mode * width : (mode + 1) * width] * weight
                    two = whole[(modes + mode) * width : (modes + mode + 1) * width] * weight
                    real = one if real is None else real + one
                    imag = two if imag is None else imag + two
                omega = values[2 + out_mode : 3 + out_mode]
                bose = 1.0 / (jnp.exp(omega / THERMAL) - 1.0)
                scale = SMEARING / math.pi
                up = spacing + omega
                off = spacing - omega
                up = up * up + SMEARING * SMEARING
                off = off * off + SMEARING * SMEARING
                absorb = (bose + fermi) * scale
                emit = (bose + 1.0 - fermi) * scale
                total = total + (real * real + imag * imag) * (absorb / up + emit / off)
    total = jnp.sum(total.T, axis=0, keepdims=True)
    out_ref[...] = total * (1.0 / (groups * queries))


def shards(
    coupling, eigvec, energies, k_coords, r_coords, degeneracy, kq_index, omega, phonon_modes
):
    groups = lax.axis_size("pb")
    holders = lax.axis_size("ka")
    bands = energies.shape[1]
    queries = kq_index.shape[1]
    modes = omega.shape[1]
    slab = coupling.reshape(coupling.shape[0], -1)
    tiles = slab.shape[1] // LANES
    place = jnp.stack([lax.axis_index("pb"), lax.axis_index("ka")])
    share = tiles // groups
    extra = -(-(share + 2 + modes * (modes + 1)) // 16) * 16 - share
    length = tiles + share + extra
    parcel = pl.pallas_call(
        functools.partial(pack_kernel, groups),
        out_shape=jax.ShapeDtypeStruct((groups * holders, length, LANES), BF16),
        in_specs=[SMEM] + [VMEM] * 9,
        out_specs=VMEM,
        scratch_shapes=[
            pltpu.VMEM((holders * tiles, LANES), F32),
            pltpu.VMEM((extra, LANES), F32),
        ],
        name="pack",
    )(
        place, k_coords, r_coords, degeneracy.reshape(1, -1), slab, eigvec.reshape(tiles, LANES),
        energies, kq_index, omega.T, phonon_modes.transpose(1, 2, 0),
    )
    got = lax.all_to_all(parcel, ("pb", "ka"), 0, 0, tiled=True)
    return pl.pallas_call(
        functools.partial(energy_kernel, groups, bands, queries),
        out_shape=jax.ShapeDtypeStruct((1, bands // groups), F32),
        in_specs=[SMEM] + [VMEM] * 3,
        out_specs=VMEM,
        scratch_shapes=[
            pltpu.VMEM((LANES // bands, holders, tiles, LANES), F32),
            pltpu.VMEM((holders, 8, LANES), F32),
            pltpu.VMEM((groups, 8, LANES), jnp.int32),
            pltpu.SMEM((groups, 8, LANES), jnp.int32),
            pltpu.SemaphoreType.DMA,
        ],
        name="energy",
    )(place, got, eigvec.reshape(2, bands, bands), energies)


def solution(mesh):
    in_specs = (
        P("ka", "pb", None),
        P("ka", None),
        P("ka", None),
        P(),
        P(None, "ka"),
        P("ka"),
        P("ka", "pb"),
        P("pb", None),
        P("pb", None, None),
    )
    out_specs = P("ka", "pb")
    return jax.shard_map(shards, mesh=mesh, in_specs=in_specs, out_specs=out_specs, check_vma=False)
```

time: 140 us -> 26.7 us (0.19)
  blocking collectives: 105 us -> 0 us
  between operations: 13.6 us -> 0.02 us
  starting transfers between devices: 0.01 us -> 7.33 us
  Pallas kernels: 0 us -> 6.16 us
  matrix products: 5.57 us -> 0 us
  local copies, waits for them, and re-layouts: 6.51 us -> 3.17 us
    unnamed x1 -> x0, blocking collectives: 63.8 us -> none
    all_gather x3 -> x0, blocking collectives: 40.9 us -> none  [the longest x1 19.1 us: shards(): lax.all_gather(energies, 'ka', axis=0, tiled=True)]
    all_to_all x0 -> x1, waiting for transfers between devices: none -> 8.39 us  [shards(): got = lax.all_to_all(parcel, ('pb', 'ka'), 0, 0, tiled=True)]
    unnamed x2 -> x0, waiting for transfers between devices: 7.35 us -> none
    all_to_all x0 -> x1, starting transfers between devices: none -> 7.33 us  [shards(): got = lax.all_to_all(parcel, ('pb', 'ka'), 0, 0, tiled=True)]
    pallas_call x0 -> x2, Pallas kernels: none -> 6.16 us  [the longest x1 3.53 us: shards(): pl.pallas_call(functools.partial(energy_kernel, groups, bands, queries),...]
    dot_general x13 -> x0, matrix products: 5.57 us -> none  [the longest x1 0.96 us: self_energy(): jnp.einsum('qam,qvan->qmvn', target[:, 1], mixed_imag, precision=HIGHEST)]
    unnamed x18 -> x5, local copies, waits for them, and re-layouts: 4.06 us -> 1.2 us
  transfers between devices with their start and end apart: 1 -> 1, of which waited for: 1 -> 1; matrix products, arithmetic and copies ran while one was open for 0% -> 7% of each run, Pallas kernels for 0% -> 0%
where the time goes in v2:
time: 26.7 us; the launch traced here: 26.4 us
  waiting for transfers between devices  8.39 us (31%)
  starting transfers between devices  7.33 us (27%)
  Pallas kernels  6.16 us (23%)
  local copies, waits for them, and re-layouts  3.17 us (12%)
  other arithmetic  1.33 us (5%)
    all_to_all x1, waiting for transfers between devices, shards(): got = lax.all_to_all(parcel, ('pb', 'ka'), 0, 0, tiled=True)  8.39 us
    all_to_all x1, starting transfers between devices, shards(): got = lax.all_to_all(parcel, ('pb', 'ka'), 0, 0, tiled=True)  7.33 us
    pallas_call x1, Pallas kernels, shards(): pl.pallas_call(functools.partial(energy_kernel, groups, bands, queries),...  3.53 us
    pallas_call x1, Pallas kernels, shards(): pl.pallas_call(functools.partial(pack_kernel, groups), out_shape=jax.Shap...  2.63 us
    reshape x1, local copies, waits for them, and re-layouts, shards(): degeneracy.reshape(1, -1)  1.29 us
    unnamed x5, local copies, waits for them, and re-layouts  1.2 us
    reshape x1, local copies, waits for them, and re-layouts, shards(): eigvec.reshape(2, bands, bands)  0.68 us
    unnamed x1, other arithmetic  0.67 us
  transfers between devices with their start and end apart: 1, of which 1 were waited for; matrix products, arithmetic and copies ran while one was open for 7% of the time, Pallas kernels for 0%

profile of v2, /device:TPU:0, one launch (start us, length us, event | category | flops | bytes accessed | tf_op | source)
XLA Modules:
  0.0 26.4 jit_solution(5662032277222810684)
XLA Ops:
  0.0 0.0 copy-start.1
  0.0 1.3 %reshape.12.degeneracy_ref = s32[1,320]{1,0:T(1,128)} reshape(s32[320]{0:T(512)} %param.14) | data formatting | bytes 2560 | tf_op jit(solution)/shard_map/reshape | solution.py:253
  1.3 0.7 %pad_add_fusion.place = s32[2]{0:T(128)} fusion(s32[1]{0:T(128)} %bitcast.1, s32[1]{0:T(128)} %bitcast), kind=kLoop, calls=%fused_computation | loop fusion | flops 2 | bytes 16 | tf_op jit(solution)/shard_map/stack | solution.py:238
  2.0 2.6 %pack.1 = bf16[32,32,128]{2,1,0:T(8,128)(2,1)} custom-call(s32[2]{0:T(128)} %pad_add_fusion.place, s32[3,16]{1,0:T(4,128)} %k_ref.1, s32[3,320]{1,0:T(4,128)} %r_ref.1, s32[1,320]{1,0:T(1,128)} %reshape.12.degeneracy_ref, bf16[320,2048]{1,0:T(8,128)(2,1)} %bitcast.6, f32[16,128]{1,0:T(8,128)} %bitcast.7, f32[1,32]{1,0:T(1,128)} %energy_ref.3, ...), custom_call_target="tpu_custom_call" | custom-call | tf_op jit(solution)/shard_map/pack/pallas_call | solution.py:242
  4.6 7.3 %all-to-all-start = ((bf16[32,32,128]{2,1,0:T(8,128)(2,1)}), bf16[32,32,128]{2,1,0:T(8,128)(2,1)S(1)}, u32[]{:S(2)}, u32[]{:S(2)}) async-start(bf16[32,32,128]{2,1,0:T(8,128)(2,1)} %pack.1), calls=%async_computation | async-start | bytes 524288 | tf_op jit(solution)/shard_map/all_to_all | solution.py:256
  11.9 0.5 %broadcast.3 = f32[]{:T(128)} broadcast(f32[]{:T(128)} %constant.18), dimensions={} | broadcast | bytes 8 | tf_op args[1]
  12.4 0.0 copy-done.1
  12.4 0.7 %reduce.3 = f32[2048]{0:T(1024)S(1)} reduce(f32[1,2048]{1,0:T(1,128)S(1)} %copy-done.1, f32[]{:T(128)} %broadcast.3), dimensions={0}, to_apply=%param.10.reduce_sub_computation.3 | reduce | bytes 16388 | tf_op args[1]
  13.1 0.7 %reshape.15.vector_ref = f32[2,32,32]{2,1,0:T(8,128)} reshape(f32[2048]{0:T(1024)S(1)} %reduce.3) | data formatting | bytes 16384 | tf_op jit(solution)/shard_map/reshape | solution.py:270
  13.8 8.4 %all-to-all-done.got_ref = bf16[32,32,128]{2,1,0:T(8,128)(2,1)S(1)} async-done(((bf16[32,32,128]{2,1,0:T(8,128)(2,1)}), bf16[32,32,128]{2,1,0:T(8,128)(2,1)S(1)}, u32[]{:S(2)}, u32[]{:S(2)}) %all-to-all-start) | async-done | bytes 262176 | tf_op jit(solution)/shard_map/all_to_all | solution.py:256
  22.2 0.0 copy-start
  22.2 0.7 %copy-done = bf16[32,32,128]{2,1,0:T(8,128)(2,1)} copy-done((bf16[32,32,128]{2,1,0:T(8,128)(2,1)}, bf16[32,32,128]{2,1,0:T(8,128)(2,1)S(1)}, u32[]{:S(2)}) %copy-start) | copy-done | bytes 262168
  22.9 3.5 %energy.1 = f32[1,16]{1,0:T(1,128)} custom-call(s32[2]{0:T(128)} %pad_add_fusion.place, bf16[32,32,128]{2,1,0:T(8,128)(2,1)} %copy-done, f32[2,32,32]{2,1,0:T(8,128)} %reshape.15.vector_ref, f32[1,32]{1,0:T(1,128)} %energy_ref.3), custom_call_target="tpu_custom_call" | custom-call | tf_op jit(solution)/shard_map/energy/pallas_call | solution.py:257
Async XLA Ops:
  0.0 12.4 %copy-start.1 = (f32[1,2048]{1,0:T(1,128)S(1)}, f32[1,2048]{1,0:T(1,128)}, u32[]{:S(2)}) copy-start(f32[1,2048]{1,0:T(1,128)} %param.10) | copy-start | bytes 24580
  4.6 17.6 %all-to-all-start = ((bf16[32,32,128]{2,1,0:T(8,128)(2,1)}), bf16[32,32,128]{2,1,0:T(8,128)(2,1)S(1)}, u32[]{:S(2)}, u32[]{:S(2)}) async-start(bf16[32,32,128]{2,1,0:T(8,128)(2,1)} %pack.1), calls=%async_computation | async-start | bytes 524288 | tf_op jit(solution)/shard_map/all_to_all | solution.py:256
  22.2 0.7 %copy-start = (bf16[32,32,128]{2,1,0:T(8,128)(2,1)}, bf16[32,32,128]{2,1,0:T(8,128)(2,1)S(1)}, u32[]{:S(2)}) copy-start(bf16[32,32,128]{2,1,0:T(8,128)(2,1)S(1)} %all-to-all-done.got_ref) | copy-start | bytes 786436

commit v3 on v2

--- a/solution.py
+++ b/solution.py
@@ -18,7 +18,6 @@
 F32 = jnp.float32
 BF16 = jnp.bfloat16
 VMEM = pl.BlockSpec(memory_space=pltpu.VMEM)
-SMEM = pl.BlockSpec(memory_space=pltpu.SMEM)
 
 
 def wave(turns):
@@ -42,9 +41,10 @@
 
 
 def pack_kernel(
-    groups, place, k_ref, r_ref, degeneracy_ref, coupling_ref, vector_ref, energy_ref,
+    groups, k_ref, r_ref, degeneracy_ref, coupling_ref, vector_ref, energy_ref,
     index_ref, omega_ref, phonon_ref, out_ref, rows_ref, extra_ref,
 ):
+    place = lax.axis_index("pb")
     count = k_ref.shape[1]
     width = coupling_ref.shape[1]
     tiles = width // LANES
@@ -54,7 +54,7 @@
         preferred_element_type=F32, precision=HIGHEST,
     ).astype(jnp.int32)
     cosine, sine = wave(turns)
-    inverse = 1.0 / degeneracy_ref[...].astype(F32)
+    inverse = 1.0 / degeneracy_ref[...].astype(F32).reshape(1, -1)
     both = jnp.concatenate([cosine * inverse, sine * inverse], axis=0).astype(BF16)
     step = 2 * LANES
     for start in range(0, width // 2, step):
@@ -83,7 +83,7 @@
     extra = jnp.where(lane < HALF, high, low)
     mine = vector_ref[0:share, :]
     for group in range(1, groups):
-        mine = jnp.where(place[0] == group, vector_ref[group * share : (group + 1) * share, :], mine)
+        mine = jnp.where(place == group, vector_ref[group * share : (group + 1) * share, :], mine)
     tail = jnp.concatenate([mine, extra], axis=0).astype(BF16)
     for row in range(count):
         block = rows_ref[row * tiles : (row + 1) * tiles, :].astype(BF16)
@@ -98,10 +98,10 @@
 
 
 def energy_kernel(
-    groups, bands, queries, place, got_ref, vector_ref, energy_ref, out_ref,
+    groups, bands, queries, got_ref, vector_ref, energy_ref, out_ref,
     turned_ref, level_ref, index_ref, scalar_ref, semaphore,
 ):
-    own_group, own_holder = place[0], place[1]
+    own_group, own_holder = lax.axis_index("pb"), lax.axis_index("ka")
     holders = got_ref.shape[0] // groups
     tiles = 2 * bands * bands // LANES
     share = tiles // groups
@@ -225,6 +225,10 @@
     out_ref[...] = total * (1.0 / (groups * queries))
 
 
+def grant(size):
+    return size + size // 4 + (2 << 20)
+
+
 def shards(
     coupling, eigvec, energies, k_coords, r_coords, degeneracy, kq_index, omega, phonon_modes
 ):
@@ -235,14 +239,13 @@
     modes = omega.shape[1]
     slab = coupling.reshape(coupling.shape[0], -1)
     tiles = slab.shape[1] // LANES
-    place = jnp.stack([lax.axis_index("pb"), lax.axis_index("ka")])
     share = tiles // groups
     extra = -(-(share + 2 + modes * (modes + 1)) // 16) * 16 - share
     length = tiles + share + extra
     parcel = pl.pallas_call(
         functools.partial(pack_kernel, groups),
         out_shape=jax.ShapeDtypeStruct((groups * holders, length, LANES), BF16),
-        in_specs=[SMEM] + [VMEM] * 9,
+        in_specs=[VMEM] * 9,
         out_specs=VMEM,
         scratch_shapes=[
             pltpu.VMEM((holders * tiles, LANES), F32),
@@ -250,14 +253,14 @@
         ],
         name="pack",
     )(
-        place, k_coords, r_coords, degeneracy.reshape(1, -1), slab, eigvec.reshape(tiles, LANES),
+        k_coords, r_coords, degeneracy, slab, eigvec.reshape(tiles, LANES),
         energies, kq_index, omega.T, phonon_modes.transpose(1, 2, 0),
     )
     got = lax.all_to_all(parcel, ("pb", "ka"), 0, 0, tiled=True)
     return pl.pallas_call(
         functools.partial(energy_kernel, groups, bands, queries),
         out_shape=jax.ShapeDtypeStruct((1, bands // groups), F32),
-        in_specs=[SMEM] + [VMEM] * 3,
+        in_specs=[VMEM] * 3,
         out_specs=VMEM,
         scratch_shapes=[
             pltpu.VMEM((LANES // bands, holders, tiles, LANES), F32),
@@ -266,8 +269,13 @@
             pltpu.SMEM((groups, 8, LANES), jnp.int32),
             pltpu.SemaphoreType.DMA,
         ],
+        compiler_params=pltpu.CompilerParams(
+            vmem_limit_bytes=grant(
+                2 * got.size + 4 * LANES * holders * (tiles * LANES // bands + 8)
+            )
+        ),
         name="energy",
-    )(place, got, eigvec.reshape(2, bands, bands), energies)
+    )(got, eigvec.reshape(2, bands, bands), energies)
 
 
 def solution(mesh):

time: 26.7 us -> 23 us (0.86)
  local copies, waits for them, and re-layouts: 3.17 us -> 0.59 us
  Pallas kernels: 6.16 us -> 5.2 us
  other arithmetic: 1.33 us -> 0.67 us
  waiting for transfers between devices: 8.39 us -> 8.99 us
    reshape x1 -> x0, local copies, waits for them, and re-layouts: 1.29 us -> none  [shards(): degeneracy.reshape(1, -1)]
    pallas_call x1, Pallas kernels: 3.53 us -> 2.55 us  [shards(): pl.pallas_call(functools.partial(energy_kernel, groups, bands, queries),...]
    unnamed x5, local copies, waits for them, and re-layouts: 1.2 us -> 0.52 us
    another operation x1 -> x0, other arithmetic: 0.66 us -> none  [shards(): place = jnp.stack([lax.axis_index('pb'), lax.axis_index('ka')])]
    all_to_all x1, waiting for transfers between devices: 8.39 us -> 8.99 us  [shards(): got = lax.all_to_all(parcel, ('pb', 'ka'), 0, 0, tiled=True)]
    reshape x1, local copies, waits for them, and re-layouts: 0.68 us -> 0.07 us  [shards(): eigvec.reshape(2, bands, bands)]
  transfers between devices with their start and end apart: 1 -> 1, of which waited for: 1 -> 1; matrix products, arithmetic and copies ran while one was open for 7% -> 5% of each run, Pallas kernels for 0% -> 0%
where the time goes in v3:
time: 23 us; the launch traced here: 22.8 us
  waiting for transfers between devices  8.99 us (39%)
  starting transfers between devices  7.32 us (32%)
  Pallas kernels  5.2 us (23%)
  other arithmetic  0.67 us (3%)
  local copies, waits for them, and re-layouts  0.59 us (3%)
    all_to_all x1, waiting for transfers between devices, shards(): got = lax.all_to_all(parcel, ('pb', 'ka'), 0, 0, tiled=True)  8.99 us
    all_to_all x1, starting transfers between devices, shards(): got = lax.all_to_all(parcel, ('pb', 'ka'), 0, 0, tiled=True)  7.32 us
    pallas_call x1, Pallas kernels, shards(): pl.pallas_call(functools.partial(pack_kernel, groups), out_shape=jax.Shap...  2.65 us
    pallas_call x1, Pallas kernels, shards(): pl.pallas_call(functools.partial(energy_kernel, groups, bands, queries),...  2.55 us
    unnamed x1, other arithmetic  0.67 us
    unnamed x5, local copies, waits for them, and re-layouts  0.52 us
  transfers between devices with their start and end apart: 1, of which 1 were waited for; matrix products, arithmetic and copies ran while one was open for 5% of the time, Pallas kernels for 0%

profile of v3, /device:TPU:0, one launch (start us, length us, event | category | flops | bytes accessed | tf_op | source)
XLA Modules:
  0.0 22.8 jit_solution(6961917196924160839)
XLA Ops:
  0.0 0.0 copy-start.1
  0.0 0.0 copy-start
  0.0 2.6 %pack.1 = bf16[32,32,128]{2,1,0:T(8,128)(2,1)} custom-call(s32[3,16]{1,0:T(4,128)} %k_ref.1, s32[3,320]{1,0:T(4,128)} %r_ref.1, s32[320]{0:T(512)} %degeneracy_ref.1, bf16[320,2048]{1,0:T(8,128)(2,1)} %bitcast.4, f32[16,128]{1,0:T(8,128)} %bitcast.5, f32[1,32]{1,0:T(1,128)} %energy_ref.3, s32[1,12]{1,0:T(1,128)} %index_ref.1, f32[2,12]{1,0:T(2,128)} %bitcast.7, ...), custom_call_target="tpu_custom_call" | custom-call | tf_op jit(solution)/shard_map/pack/pallas_call | solution.py:245
  2.7 7.3 %all-to-all-start = ((bf16[32,32,128]{2,1,0:T(8,128)(2,1)}), bf16[32,32,128]{2,1,0:T(8,128)(2,1)S(1)}, u32[]{:S(2)}, u32[]{:S(2)}) async-start(bf16[32,32,128]{2,1,0:T(8,128)(2,1)} %pack.1), calls=%async_computation | async-start | bytes 524288 | tf_op jit(solution)/shard_map/all_to_all | solution.py:259
  10.0 0.5 %broadcast.3 = f32[]{:T(128)} broadcast(f32[]{:T(128)} %constant.7), dimensions={} | broadcast | bytes 8 | tf_op args[1]
  10.5 0.0 copy-done.1
  10.5 0.7 %reduce.3 = f32[2048]{0:T(1024)S(1)} reduce(f32[1,2048]{1,0:T(1,128)S(1)} %copy-done.1, f32[]{:T(128)} %broadcast.3), dimensions={0}, to_apply=%param.10.reduce_sub_computation.3 | reduce | bytes 16388 | tf_op args[1]
  11.2 0.1 reshape.11.vector_ref
  11.2 9.0 %all-to-all-done.got_ref = bf16[32,32,128]{2,1,0:T(8,128)(2,1)S(1)} async-done(((bf16[32,32,128]{2,1,0:T(8,128)(2,1)}), bf16[32,32,128]{2,1,0:T(8,128)(2,1)S(1)}, u32[]{:S(2)}, u32[]{:S(2)}) %all-to-all-start) | async-done | bytes 262176 | tf_op jit(solution)/shard_map/all_to_all | solution.py:259
  20.2 0.0 copy-done
  20.2 2.6 %energy.1 = f32[1,16]{1,0:T(1,128)} custom-call(bf16[32,32,128]{2,1,0:T(8,128)(2,1)S(1)} %all-to-all-done.got_ref, f32[2,32,32]{2,1,0:T(8,128)S(1)} %reshape.11.vector_ref, f32[1,32]{1,0:T(1,128)S(1)} %copy-done), custom_call_target="tpu_custom_call" | custom-call | tf_op jit(solution)/shard_map/energy/pallas_call | solution.py:260
Async XLA Ops:
  0.0 10.5 %copy-start.1 = (f32[1,2048]{1,0:T(1,128)S(1)}, f32[1,2048]{1,0:T(1,128)}, u32[]{:S(2)}) copy-start(f32[1,2048]{1,0:T(1,128)} %param.10) | copy-start | bytes 24580
  0.0 20.2 %copy-start = (f32[1,32]{1,0:T(1,128)S(1)}, f32[1,32]{1,0:T(1,128)}, u32[]{:S(2)}) copy-start(f32[1,32]{1,0:T(1,128)} %energy_ref.3) | copy-start | bytes 388
  2.7 17.6 %all-to-all-start = ((bf16[32,32,128]{2,1,0:T(8,128)(2,1)}), bf16[32,32,128]{2,1,0:T(8,128)(2,1)S(1)}, u32[]{:S(2)}, u32[]{:S(2)}) async-start(bf16[32,32,128]{2,1,0:T(8,128)(2,1)} %pack.1), calls=%async_computation | async-start | bytes 524288 | tf_op jit(solution)/shard_map/all_to_all | solution.py:259

commit v4 on v3

--- a/solution.py
+++ b/solution.py
@@ -11,12 +11,14 @@
 KGRID = 64
 LANES = 128
 HALF = LANES // 2
+CHUNKS = 4
 
 THERMAL = 0.1
 SMEARING = 0.05
 HIGHEST = lax.Precision.HIGHEST
 F32 = jnp.float32
 BF16 = jnp.bfloat16
+HBM = pl.BlockSpec(memory_space=pltpu.HBM)
 VMEM = pl.BlockSpec(memory_space=pltpu.VMEM)
 
 
@@ -56,18 +58,6 @@
     cosine, sine = wave(turns)
     inverse = 1.0 / degeneracy_ref[...].astype(F32).reshape(1, -1)
     both = jnp.concatenate([cosine * inverse, sine * inverse], axis=0).astype(BF16)
-    step = 2 * LANES
-    for start in range(0, width // 2, step):
-        left = jnp.dot(both, coupling_ref[:, start : start + step], preferred_element_type=F32)
-        other = start + width // 2
-        right = jnp.dot(both, coupling_ref[:, other : other + step], preferred_element_type=F32)
-        real = left[:count] - right[count:]
-        imag = right[:count] + left[count:]
-        for piece in range(step // LANES):
-            tile = start // LANES + piece
-            lanes = slice(piece * LANES, (piece + 1) * LANES)
-            rows_ref[pl.ds(tile, count, tiles), :] = real[:, lanes]
-            rows_ref[pl.ds(tile + tiles // 2, count, tiles), :] = imag[:, lanes]
     extra_ref[...] = jnp.zeros_like(extra_ref)
     bands, queries, modes = energy_ref.shape[1], index_ref.shape[1], omega_ref.shape[0]
     extra_ref[0:1, :bands] = energy_ref[...]
@@ -85,6 +75,18 @@
     for group in range(1, groups):
         mine = jnp.where(place == group, vector_ref[group * share : (group + 1) * share, :], mine)
     tail = jnp.concatenate([mine, extra], axis=0).astype(BF16)
+    step = 2 * LANES
+    for start in range(0, width // 2, step):
+        left = jnp.dot(both, coupling_ref[:, start : start + step], preferred_element_type=F32)
+        other = start + width // 2
+        right = jnp.dot(both, coupling_ref[:, other : other + step], preferred_element_type=F32)
+        real = left[:count] - right[count:]
+        imag = right[:count] + left[count:]
+        for piece in range(step // LANES):
+            tile = start // LANES + piece
+            lanes = slice(piece * LANES, (piece + 1) * LANES)
+            rows_ref[pl.ds(tile, count, tiles), :] = real[:, lanes]
+            rows_ref[pl.ds(tile + tiles // 2, count, tiles), :] = imag[:, lanes]
     for row in range(count):
         block = rows_ref[row * tiles : (row + 1) * tiles, :].astype(BF16)
         for group in range(groups):
@@ -99,7 +101,7 @@
 
 def energy_kernel(
     groups, bands, queries, got_ref, vector_ref, energy_ref, out_ref,
-    turned_ref, level_ref, index_ref, scalar_ref, semaphore,
+    turned_ref, level_ref, flat_ref, index_ref, scalar_ref, semaphore,
 ):
     own_group, own_holder = lax.axis_index("pb"), lax.axis_index("ka")
     holders = got_ref.shape[0] // groups
@@ -127,10 +129,17 @@
             for piece in range(fold):
                 stack.append(block[:, piece * bands : (piece + 1) * bands])
     matrix = jnp.concatenate(stack, axis=0)
-    vector = vector_ref[:, :, :width]
-    for group in range(1, groups):
-        other = vector_ref[:, :, group * width : (group + 1) * width]
-        vector = jnp.where(own_group == group, other, vector)
+    vector = []
+    for part in range(2):
+        block = vector_ref[part * half : (part + 1) * half, :]
+        for piece in range(fold):
+            first = piece * bands
+            value = block[:, first : first + width]
+            for group in range(1, groups):
+                other = block[:, first + group * width : first + (group + 1) * width]
+                value = jnp.where(own_group == group, other, value)
+            flat_ref[part, pl.ds(piece, half, fold), :width] = value
+        vector.append(flat_ref[part, :, :width])
     with_real = jnp.dot(matrix, vector[0], precision=HIGHEST, preferred_element_type=F32)
     with_imag = jnp.dot(matrix, vector[1], precision=HIGHEST, preferred_element_type=F32)
     reals, imags = [], []
@@ -242,6 +251,11 @@
     share = tiles // groups
     extra = -(-(share + 2 + modes * (modes + 1)) // 16) * 16 - share
     length = tiles + share + extra
+    operands = (
+        k_coords, r_coords, degeneracy, slab, eigvec.reshape(tiles, LANES),
+        energies, kq_index, omega.T, phonon_modes.transpose(1, 2, 0),
+    )
+    operands = tuple(pltpu.with_memory_space_constraint(x, pltpu.HBM) for x in operands)
     parcel = pl.pallas_call(
         functools.partial(pack_kernel, groups),
         out_shape=jax.ShapeDtypeStruct((groups * holders, length, LANES), BF16),
@@ -251,11 +265,12 @@
             pltpu.VMEM((holders * tiles, LANES), F32),
             pltpu.VMEM((extra, LANES), F32),
         ],
+        compiler_params=pltpu.CompilerParams(
+            vmem_limit_bytes=grant(2 * (slab.size + groups * holders * length * LANES))
+            + 4 * holders * tiles * LANES
+        ),
         name="pack",
-    )(
-        k_coords, r_coords, degeneracy, slab, eigvec.reshape(tiles, LANES),
-        energies, kq_index, omega.T, phonon_modes.transpose(1, 2, 0),
-    )
+    )(*operands)
     got = lax.all_to_all(parcel, ("pb", "ka"), 0, 0, tiled=True)
     return pl.pallas_call(
         functools.partial(energy_kernel, groups, bands, queries),
@@ -265,6 +280,7 @@
         scratch_shapes=[
             pltpu.VMEM((LANES // bands, holders, tiles, LANES), F32),
             pltpu.VMEM((holders, 8, LANES), F32),
+            pltpu.VMEM((2, bands, LANES), F32),
             pltpu.VMEM((groups, 8, LANES), jnp.int32),
             pltpu.SMEM((groups, 8, LANES), jnp.int32),
             pltpu.SemaphoreType.DMA,
@@ -275,7 +291,7 @@
             )
         ),
         name="energy",
-    )(got, eigvec.reshape(2, bands, bands), energies)
+    )(got, eigvec.reshape(tiles, LANES), energies)
 
 
 def solution(mesh):

time: 23 us -> 22 us (0.957)
  blocking collectives: 0 us -> 17.4 us
  waiting for transfers between devices: 8.99 us -> 0 us
  starting transfers between devices: 7.32 us -> 0 us
  Pallas kernels: 5.2 us -> 4.48 us
  other arithmetic: 0.67 us -> 0 us
  local copies, waits for them, and re-layouts: 0.59 us -> 0.01 us
    all_to_all x0 -> x1, blocking collectives: none -> 17.4 us  [shards(): got = lax.all_to_all(parcel, ('pb', 'ka'), 0, 0, tiled=True)]
    all_to_all x1 -> x0, waiting for transfers between devices: 8.99 us -> none  [shards(): got = lax.all_to_all(parcel, ('pb', 'ka'), 0, 0, tiled=True)]
    all_to_all x1 -> x0, starting transfers between devices: 7.32 us -> none  [shards(): got = lax.all_to_all(parcel, ('pb', 'ka'), 0, 0, tiled=True)]
    pallas_call x1, Pallas kernels: 2.65 us -> 1.96 us  [shards(): pl.pallas_call(functools.partial(pack_kernel, groups), out_shape=jax.Shap...]
    unnamed x1 -> x0, other arithmetic: 0.67 us -> none
    unnamed x5 -> x4, local copies, waits for them, and re-layouts: 0.52 us -> 0.01 us
  transfers between devices with their start and end apart: 1 -> 0, of which waited for: 1 -> 0; matrix products, arithmetic and copies ran while one was open for 5% -> 0% of each run, Pallas kernels for 0% -> 0%
where the time goes in v4:
time: 22 us; the launch traced here: 21.9 us
  blocking collectives  17.4 us (79%)
  Pallas kernels  4.48 us (20%)
    all_to_all x1, blocking collectives, shards(): got = lax.all_to_all(parcel, ('pb', 'ka'), 0, 0, tiled=True)  17.4 us
    pallas_call x1, Pallas kernels, shards(): pl.pallas_call(functools.partial(energy_kernel, groups, bands, queries),...  2.53 us
    pallas_call x1, Pallas kernels, shards(): pl.pallas_call(functools.partial(pack_kernel, groups), out_shape=jax.Shap...  1.96 us

profile of v4, /device:TPU:0, one launch (start us, length us, event | category | flops | bytes accessed | tf_op | source)
XLA Modules:
  0.0 21.9 jit_solution(14548935842088547033)
XLA Ops:
  0.0 0.0 copy-start.1
  0.0 0.0 copy-start
  0.0 2.0 %pack.1 = bf16[32,32,128]{2,1,0:T(8,128)(2,1)S(1)} custom-call(s32[3,16]{1,0:T(4,128)} %k_ref.1, s32[3,320]{1,0:T(4,128)} %r_ref.1, s32[320]{0:T(512)} %degeneracy_ref.1, bf16[320,2048]{1,0:T(8,128)(2,1)} %bitcast.6, f32[16,128]{1,0:T(8,128)} %bitcast.4, f32[1,32]{1,0:T(1,128)} %energy_ref.3, s32[1,12]{1,0:T(1,128)} %index_ref.1, f32[2,12]{1,0:T(2,128)} %bitcast.8, ...), custom_call_target="tpu_custom_call" | custom-call | tf_op jit(solution)/shard_map/pack/pallas_call | solution.py:259
  2.0 17.4 %all_to_all.5.got_ref = bf16[32,32,128]{2,1,0:T(8,128)(2,1)S(1)} all-to-all(bf16[32,32,128]{2,1,0:T(8,128)(2,1)S(1)} %pack.1), channel_id=1, replica_groups=mesh['pb'=2,'ka'=16] {'pb','ka'}, dimensions={0} | all-to-all | bytes 524288 | tf_op jit(solution)/shard_map/all_to_all | solution.py:274
  19.4 0.0 copy-done.1
  19.4 0.0 copy-done
  19.4 2.5 %energy.1 = f32[1,16]{1,0:T(1,128)} custom-call(bf16[32,32,128]{2,1,0:T(8,128)(2,1)S(1)} %all_to_all.5.got_ref, f32[16,128]{1,0:T(8,128)S(1)} %bitcast.5, f32[1,32]{1,0:T(1,128)S(1)} %copy-done.1), custom_call_target="tpu_custom_call" | custom-call | tf_op jit(solution)/shard_map/energy/pallas_call | solution.py:275
Async XLA Ops:
  0.0 19.4 %copy-start.1 = (f32[1,32]{1,0:T(1,128)S(1)}, f32[1,32]{1,0:T(1,128)}, u32[]{:S(2)}) copy-start(f32[1,32]{1,0:T(1,128)} %energy_ref.3) | copy-start | bytes 388
  0.0 19.4 %copy-start = (f32[1,2048]{1,0:T(1,128)S(1)}, f32[1,2048]{1,0:T(1,128)}, u32[]{:S(2)}) copy-start(f32[1,2048]{1,0:T(1,128)} %param.10) | copy-start | bytes 24580

commit v5 on v4

--- a/solution.py
+++ b/solution.py
@@ -42,18 +42,31 @@
     return cosine, sine
 
 
-def pack_kernel(
-    groups, k_ref, r_ref, degeneracy_ref, coupling_ref, vector_ref, energy_ref,
-    index_ref, omega_ref, phonon_ref, out_ref, rows_ref, extra_ref,
-):
+def pack_kernel(groups, *refs):
+    sources, out_ref, (rows_ref, extra_ref) = refs[:9], refs[9], refs[10:12]
+    copies, semaphores = refs[12:21], refs[21]
+    k_ref, r_ref, degeneracy_ref, coupling_ref, vector_ref, energy_ref = copies[:6]
+    index_ref, omega_ref, phonon_ref = copies[6:]
+    pending = [
+        pltpu.make_async_copy(source, target, semaphores.at[number])
+        for number, (source, target) in enumerate(zip(sources, copies, strict=True))
+    ]
+    slab_copy = pending.pop(3)
+    for copy in pending[:3]:
+        copy.start()
+    slab_copy.start()
+    for copy in pending[3:]:
+        copy.start()
+    for copy in pending:
+        copy.wait()
     place = lax.axis_index("pb")
     count = k_ref.shape[1]
     width = coupling_ref.shape[1]
     tiles = width // LANES
     share = tiles // groups
     turns = lax.dot_general(
-        k_ref[...].astype(F32), r_ref[...].astype(F32), (((0,), (0,)), ((), ())),
-        preferred_element_type=F32, precision=HIGHEST,
+        k_ref[...].astype(F32).astype(BF16), r_ref[...].astype(F32).astype(BF16),
+        (((0,), (0,)), ((), ())), preferred_element_type=F32,
     ).astype(jnp.int32)
     cosine, sine = wave(turns)
     inverse = 1.0 / degeneracy_ref[...].astype(F32).reshape(1, -1)
@@ -75,6 +88,7 @@
     for group in range(1, groups):
         mine = jnp.where(place == group, vector_ref[group * share : (group + 1) * share, :], mine)
     tail = jnp.concatenate([mine, extra], axis=0).astype(BF16)
+    slab_copy.wait()
     step = 2 * LANES
     for start in range(0, width // 2, step):
         left = jnp.dot(both, coupling_ref[:, start : start + step], preferred_element_type=F32)
@@ -112,23 +126,17 @@
     modes = groups
     width = bands // groups
     begin = tiles + share
-    for group in range(groups):
-        row = got_ref[group * holders + own_holder, begin : begin + 8, :].astype(F32)
-        index_ref[group] = row.astype(jnp.int32)
     copy = pltpu.make_async_copy(index_ref, scalar_ref, semaphore)
-    copy.start()
+
+    @pl.when(own_holder >= 0)
+    def _():
+        for group in range(groups):
+            row = got_ref[group * holders + own_holder, begin : begin + 8, :].astype(F32)
+            index_ref[group] = row.astype(jnp.int32)
+        copy.start()
+
     lane = lax.broadcasted_iota(jnp.int32, (8, LANES), 1)
     slot = lane // bands
-    stack = []
-    for mode in range(modes):
-        total = got_ref[mode * holders, :tiles, :].astype(F32)
-        for holder in range(1, holders):
-            total = total + got_ref[mode * holders + holder, :tiles, :].astype(F32)
-        for part in range(2):
-            block = total[part * half : (part + 1) * half]
-            for piece in range(fold):
-                stack.append(block[:, piece * bands : (piece + 1) * bands])
-    matrix = jnp.concatenate(stack, axis=0)
     vector = []
     for part in range(2):
         block = vector_ref[part * half : (part + 1) * half, :]
@@ -139,24 +147,33 @@
                 other = block[:, first + group * width : first + (group + 1) * width]
                 value = jnp.where(own_group == group, other, value)
             flat_ref[part, pl.ds(piece, half, fold), :width] = value
-        vector.append(flat_ref[part, :, :width])
-    with_real = jnp.dot(matrix, vector[0], precision=HIGHEST, preferred_element_type=F32)
-    with_imag = jnp.dot(matrix, vector[1], precision=HIGHEST, preferred_element_type=F32)
-    reals, imags = [], []
+        vector.append(flat_ref[part, :, :width].T)
+    vector_high, vector_low = split(jnp.concatenate(vector, axis=0))
+    stack = [[], []]
     for mode in range(modes):
-        top = slice(2 * mode * bands, (2 * mode + 1) * bands)
-        low = slice((2 * mode + 1) * bands, (2 * mode + 2) * bands)
-        reals.append(with_real[top] - with_imag[low])
-        imags.append(with_imag[top] + with_real[low])
-    folded = jnp.concatenate(
-        [
-            jnp.concatenate(reals + imags, axis=1),
-            jnp.concatenate(imags + [-x for x in reals], axis=1),
-        ],
-        axis=0,
-    )
-    left = folded.T
-    left_high, left_low = split(left)
+        total = got_ref[mode * holders, :tiles, :].astype(F32)
+        for holder in range(1, holders):
+            total = total + got_ref[mode * holders + holder, :tiles, :].astype(F32)
+        for part in range(2):
+            block = total[part * half : (part + 1) * half]
+            for piece in range(fold):
+                stack[part].append(block[:, piece * bands : (piece + 1) * bands])
+    matrix_high, matrix_low = split(jnp.concatenate(stack[0] + stack[1], axis=0))
+
+    def product(x, y):
+        return lax.dot_general(x, y, (((1,), (1,)), ((), ())), preferred_element_type=F32)
+
+    folded = product(vector_high, matrix_high) + (
+        product(vector_low, matrix_high) + product(vector_high, matrix_low)
+    )
+    side = modes * bands
+    column = lax.broadcasted_iota(jnp.int32, (width, 2 * side), 1)
+    sign = jnp.where(column < side, -1.0, 1.0)
+    first = folded[:width] + sign * pltpu.roll(folded[width:], side, 1)
+    second = pltpu.roll(first, side, 1) * -sign
+    owner = (column % side) // bands
+    left = [jnp.where(owner == mode, x, 0.0) for x in (first, second) for mode in range(modes)]
+    left_high, left_low = split(jnp.concatenate(left, axis=0))
     for holder in range(holders):
         tile = [
             got_ref[group * holders + holder, tiles : tiles + share, :].astype(F32)
@@ -166,13 +183,13 @@
         turned_ref[0, holder] = tile
         for turn in range(1, fold):
             turned_ref[turn, holder] = pltpu.roll(tile, turn * bands, 1)
-        row = got_ref[holder, begin : begin + 8, :].astype(F32)
-        row = jnp.where(lane < HALF, row + pltpu.roll(row, HALF, 1), 0.0)
-        row = jnp.where(slot < 1, row, 0.0)
-        full = row
-        for turn in range(1, fold):
-            full = full + pltpu.roll(row, turn * bands, 1)
-        level_ref[holder] = full
+    source = lax.broadcasted_iota(jnp.int32, (LANES, LANES), 0) % HALF
+    target = lax.broadcasted_iota(jnp.int32, (LANES, LANES), 1) % bands
+    spread = jnp.where(source == target, 1.0, 0.0).astype(BF16)
+    rows = [got_ref[holder, begin : begin + 8, :] for holder in range(holders)]
+    level_ref[...] = jnp.dot(
+        jnp.concatenate(rows, axis=0), spread, preferred_element_type=F32
+    ).reshape(level_ref.shape)
     span = queries * bands
     source = lax.broadcasted_iota(jnp.int32, (LANES, span), 0) % HALF
     target = lax.broadcasted_iota(jnp.int32, (LANES, span), 1) // bands
@@ -194,6 +211,7 @@
             level = level[0:1]
             blocks = []
             for part in range(2):
+                column = []
                 for piece in range(fold):
                     rows = slice(part * half, (part + 1) * half)
                     block = turned_ref[(-piece) % fold, points[0], rows, :]
@@ -203,7 +221,8 @@
                             turned_ref[(item - piece) % fold, points[item], rows, :],
                             block,
                         )
-                    blocks.append(block)
+                    column.append(block)
+                blocks += column * modes
             chosen = jnp.concatenate(blocks, axis=0).astype(BF16)
             whole = jnp.dot(left_high, chosen, preferred_element_type=F32) + jnp.dot(
                 left_low, chosen, preferred_element_type=F32
@@ -259,11 +278,13 @@
     parcel = pl.pallas_call(
         functools.partial(pack_kernel, groups),
         out_shape=jax.ShapeDtypeStruct((groups * holders, length, LANES), BF16),
-        in_specs=[VMEM] * 9,
+        in_specs=[HBM] * 9,
         out_specs=VMEM,
         scratch_shapes=[
             pltpu.VMEM((holders * tiles, LANES), F32),
             pltpu.VMEM((extra, LANES), F32),
+            *(pltpu.VMEM(x.shape, x.dtype) for x in operands),
+            pltpu.SemaphoreType.DMA((9,)),
         ],
         compiler_params=pltpu.CompilerParams(
             vmem_limit_bytes=grant(2 * (slab.size + groups * holders * length * LANES))

time: 22 us -> 21 us (0.955)
  Pallas kernels: 4.48 us -> 3.44 us
    pallas_call x1, Pallas kernels: 2.53 us -> 1.6 us  [shards(): pl.pallas_call(functools.partial(energy_kernel, groups, bands, queries),...]
where the time goes in v5:
time: 21 us; the launch traced here: 20.8 us
  blocking collectives  17.4 us (83%)
  Pallas kernels  3.44 us (16%)
    all_to_all x1, blocking collectives, shards(): got = lax.all_to_all(parcel, ('pb', 'ka'), 0, 0, tiled=True)  17.4 us
    pallas_call x1, Pallas kernels, shards(): pl.pallas_call(functools.partial(pack_kernel, groups), out_shape=jax.Shap...  1.84 us
    pallas_call x1, Pallas kernels, shards(): pl.pallas_call(functools.partial(energy_kernel, groups, bands, queries),...  1.6 us

profile of v5, /device:TPU:0, one launch (start us, length us, event | category | flops | bytes accessed | tf_op | source)
XLA Modules:
  0.0 20.8 jit_solution(6536503096478735970)
XLA Ops:
  0.0 0.0 copy-start.1
  0.0 0.0 copy-start
  0.0 1.8 %pack.1 = bf16[32,32,128]{2,1,0:T(8,128)(2,1)S(1)} custom-call(s32[3,16]{1,0:T(4,128)} %refs_0_.1, s32[3,320]{1,0:T(4,128)} %refs_1_.1, s32[320]{0:T(512)} %refs_2_.1, bf16[320,2048]{1,0:T(8,128)(2,1)} %bitcast.6, f32[16,128]{1,0:T(8,128)} %bitcast.4, f32[1,32]{1,0:T(1,128)} %energy_ref.1, s32[1,12]{1,0:T(1,128)} %refs_6_.1, f32[2,12]{1,0:T(2,128)} %bitcast.8, ...), custom_call_target="tpu_custom_call" | custom-call | tf_op jit(solution)/shard_map/pack/pallas_call | solution.py:278
  1.9 17.4 %all_to_all.5.got_ref = bf16[32,32,128]{2,1,0:T(8,128)(2,1)S(1)} all-to-all(bf16[32,32,128]{2,1,0:T(8,128)(2,1)S(1)} %pack.1), channel_id=1, replica_groups=mesh['pb'=2,'ka'=16] {'pb','ka'}, dimensions={0} | all-to-all | bytes 524288 | tf_op jit(solution)/shard_map/all_to_all | solution.py:295
  19.2 0.0 copy-done.1
  19.2 0.0 copy-done
  19.2 1.6 %energy.1 = f32[1,16]{1,0:T(1,128)} custom-call(bf16[32,32,128]{2,1,0:T(8,128)(2,1)S(1)} %all_to_all.5.got_ref, f32[16,128]{1,0:T(8,128)S(1)} %bitcast.5, f32[1,32]{1,0:T(1,128)S(1)} %copy-done.1), custom_call_target="tpu_custom_call" | custom-call | tf_op jit(solution)/shard_map/energy/pallas_call | solution.py:296
Async XLA Ops:
  0.0 19.2 %copy-start.1 = (f32[1,32]{1,0:T(1,128)S(1)}, f32[1,32]{1,0:T(1,128)}, u32[]{:S(2)}) copy-start(f32[1,32]{1,0:T(1,128)} %energy_ref.1) | copy-start | bytes 388
  0.0 19.2 %copy-start = (f32[1,2048]{1,0:T(1,128)S(1)}, f32[1,2048]{1,0:T(1,128)}, u32[]{:S(2)}) copy-start(f32[1,2048]{1,0:T(1,128)} %param.10) | copy-start | bytes 24580
